TPU v7x, 128 devices: a whole 4x4x4 slice. The times are simulated.
128 devices in a mesh: owner: 4 (over y), worker: 32 (over x, z, core).
Axes of the slice: x: 4, y: 4, z: 4, core: 2. Of those that a mesh axis runs over, the one named last changes fastest.
Arguments:
- states: float32 [262144, 512], P(('owner', 'worker')), may hold values from -3 to 3
- row_of_user: int32 [262144], replicated, may hold values from 0 to 262143, as said below
- event_users: int32 [65536], P(('owner', 'worker')), may hold values from 0 to 262143, as said below
- event_features: int32 [65536], P(('owner', 'worker')), may hold values from 0 to 4095
- feature_table: bfloat16 [4096, 512], replicated, may hold values from -6 to 6
- gate_in: bfloat16 [512, 1536], replicated, may hold values from -0.25 to 0.25
- gate_state: bfloat16 [512, 1536], replicated, may hold values from -0.25 to 0.25
- tower_in: bfloat16 [4096, 1024], P(('owner', 'worker')), may hold values from -0.1875 to 0.1875
- tower_out: bfloat16 [512, 4096], P(('owner', 'worker')), may hold values from -0.09375 to 0.09375
Outputs:
- new_states: float32 [262144, 512], P(('owner', 'worker'))
- scores: float32 [65536], P(('owner', 'worker'))
Inputs may be any that keep to these rules, and one draw needn't show every extreme that they name: `row_of_user`: A permutation: each user has its own state row. `event_users`: among the 512 events of one device, at most 8 have their row (row_of_user of the user) in one device's block of 2048 rows, and for every device some block receives exactly 8 of its events.
All inputs are finite; a program needn't handle non-finite values.
Results may differ from a plain program's by a relative error of at most 0.0034.
Values may be sent and summed in bfloat16 or wider, within the bound.
A program may use at most 128 MiB of HBM per device.

v0:
```python
import jax
import jax.numpy as jnp
from jax import lax
from jax.sharding import PartitionSpec as P

AXES = ("owner", "worker")


def gru_cell(inputs, prior, gate_in, gate_state):
    gx = jnp.dot(inputs, gate_in, preferred_element_type=jnp.float32)
    gh = jnp.dot(prior, gate_state, preferred_element_type=jnp.float32)
    width = prior.shape[-1]
    reset = jax.nn.sigmoid(gx[:, :width] + gh[:, :width])
    update = jax.nn.sigmoid(gx[:, width : 2 * width] + gh[:, width : 2 * width])
    cand = jnp.tanh(gx[:, 2 * width :] + reset * gh[:, 2 * width :])
    return (1.0 - update) * cand + update * prior.astype(jnp.float32)


def per_device(
    states,
    row_of_user,
    event_users,
    event_features,
    feature_table,
    gate_in,
    gate_state,
    tower_in,
    tower_out,
):
    shards = lax.axis_size(AXES)
    events = event_users.shape[0]
    row_count, width = states.shape
    cap = 2 * (events // shards)
    rows = row_of_user[event_users]
    target = rows // row_count
    local = rows - target * row_count
    hits = (target[:, None] == jnp.arange(shards, dtype=jnp.int32)[None, :]).astype(jnp.int32)
    rank = jnp.sum((jnp.cumsum(hits, axis=0) - hits) * hits, axis=1)
    slot = target * cap + rank
    packed = local + row_count * event_features
    requests = jnp.full((shards * cap,), -1, jnp.int32).at[slot].set(packed).reshape(shards, cap)
    asked = lax.all_to_all(requests, AXES, split_axis=0, concat_axis=0, tiled=True).reshape(-1)
    valid = asked >= 0
    owned = jnp.where(valid, asked, 0)
    owned_feature = owned // row_count
    owned_row = owned - owned_feature * row_count
    prior = states[owned_row].astype(jnp.bfloat16)
    inputs = feature_table[owned_feature]
    fresh = gru_cell(inputs, prior, gate_in, gate_state)
    delta = fresh - prior.astype(jnp.float32)
    ids = jnp.where(valid, owned_row, row_count)
    total = jax.ops.segment_sum(delta, ids, num_segments=row_count + 1)[:row_count]
    count = jax.ops.segment_sum(valid.astype(jnp.int32), ids, num_segments=row_count + 1)[
        :row_count
    ]
    new_states = states + total / jnp.maximum(count, 1).astype(jnp.float32)[:, None]
    joined = jnp.concatenate([fresh.astype(jnp.bfloat16), inputs], axis=1)
    hidden = jax.nn.gelu(
        lax.dot_general(
            joined,
            lax.all_gather(tower_in, AXES, axis=0, tiled=True),
            (((1,), (1,)), ((), ())),
            preferred_element_type=jnp.float32,
        )
    ).astype(jnp.bfloat16)
    tower = lax.dot_general(
        hidden,
        lax.all_gather(tower_out, AXES, axis=0, tiled=True),
        (((1,), (1,)), ((), ())),
        preferred_element_type=jnp.float32,
    )
    scored = jnp.sum(tower * inputs.astype(jnp.float32), axis=1) / jnp.sqrt(jnp.float32(width))
    back = lax.all_to_all(
        scored.reshape(shards, cap), AXES, split_axis=0, concat_axis=0, tiled=True
    )
    return (new_states, back.reshape(-1)[slot])


def solution(mesh):
    placed = (P(AXES, None), P(), P(AXES), P(AXES), P(), P(), P(), P(AXES, None), P(AXES, None))
    return jax.shard_map(
        per_device, mesh=mesh, in_specs=placed, out_specs=(P(AXES, None), P(AXES)), check_vma=False
    )
```

profile of v0, /device:TPU:1, one launch (start us, length us, event | category | flops | bytes accessed | tf_op | source)
XLA Modules:
  0.0 198.0 jit_solution(6553455652774412179)
XLA Ops:
  8.0 0.7 all-gather.4.cloned.1.call-update
  9.4 6.5 %gather_fusion = s32[512]{0:T(512)S(1)} fusion(s32[262144]{0:T(1024)} %param.10, s32[1024]{0:T(1024)S(1)} %pad_clamp_fusion.1), kind=kCustom, calls=%fused_computation | custom fusion | bytes 6144 | tf_op jit(solution)/shard_map/gather | solution.py:34
  16.6 2.4 %scatter_custom_fusion = s32[1024]{0:T(1024)S(1)} fusion(s32[512]{0:T(512)S(1)} %bitcast.51, s32[512]{0:T(512)S(1)} %get-tuple-element.10, s32[]{:T(128)} %constant.20.clone.1), kind=kCustom, calls=%fused_computation.94 | custom fusion | bytes 4100 | tf_op jit(solution)/shard_map/scatter | solution.py:41
  19.1 0.7 all_to_all.10
  19.8 11.5 %all-to-all-start = ((s32[128,1,8]{2,1,0:T(1,128)}), s32[128,1,8]{2,1,0:T(1,128)S(1)}, u32[]{:S(2)}, u32[]{:S(2)}) async-start(s32[128,1,8]{2,1,0:T(1,128)} %bitcast.7), calls=%async_computation | async-start | bytes 131072 | tf_op jit(solution)/shard_map/all_to_all | solution.py:42
  31.3 9.3 %all-to-all-done = s32[128,1,8]{2,1,0:T(1,128)S(1)} async-done(((s32[128,1,8]{2,1,0:T(1,128)}), s32[128,1,8]{2,1,0:T(1,128)S(1)}, u32[]{:S(2)}, u32[]{:S(2)}) %all-to-all-start) | async-done | bytes 4128 | tf_op jit(solution)/shard_map/all_to_all | solution.py:42
  41.1 1.0 fusion.44
  42.4 6.7 %gather_fusion.1 = bf16[1024,512]{1,0:T(8,128)(2,1)S(1)} fusion(bf16[4096,512]{1,0:T(8,128)(2,1)} %param.13, s32[1024]{0:T(1024)S(1)} %broadcast_clamp_fusion.1), kind=kCustom, calls=%fused_computation.1 | custom fusion | bytes 2101248 | tf_op jit(solution)/shard_map/gather | solution.py:48
  49.1 1.3 copy.18
  50.5 7.5 %gather_fusion.2 = f32[1024,512]{1,0:T(8,128)} fusion(f32[2048,512]{1,0:T(8,128)} %param.9, s32[1024]{0:T(1024)S(1)} %broadcast_clamp_fusion), kind=kCustom, calls=%fused_computation.2 | custom fusion | bytes 4198400 | tf_op jit(solution)/shard_map/gather | solution.py:47
  57.9 6.9 %scatter_custom_fusion.2 = s32[2049]{0:T(1024)S(1)} fusion(s32[1024]{0:T(1024)S(1)} %bitcast.53, s32[1024]{0:T(1024)S(1)} %reshape.288, s32[]{:T(128)} %constant.21.clone.1), kind=kCustom, calls=%fused_computation.66 | custom fusion | flops 1024 | bytes 8200 | tf_op jit(solution)/shard_map/scatter-add | solution.py:53
  64.9 1.8 fusion.66
  66.9 1.8 fusion.61
  68.7 3.1 %fusion.64 = (bf16[1024,512]{1,0:T(8,128)(2,1)}, f32[1024,512]{1,0:T(8,128)}) fusion(f32[1024,512]{1,0:T(8,128)S(1)} %copy-done.1, f32[1024,1536]{1,0:T(8,128)S(1)} %fusion.61, f32[1024,1536]{1,0:T(8,128)S(1)} %fusion.66), kind=kLoop, calls=%fused_computation.106 | loop fusion | flops 8912896 | bytes 17825792 | tf_op jit(solution)/shard_map/convert_element_type | solution.py:57
  71.8 10.3 %scatter_custom_fusion.1 = f32[2049,512]{1,0:T(8,128)} fusion(s32[1024]{0:T(1024)S(1)} %bitcast.54, f32[]{:T(128)} %constant.19.clone.1, f32[1024,512]{1,0:T(8,128)} %get-tuple-element.5, f32[1024,512]{1,0:T(8,128)} %gather_fusion.2), kind=kCustom, calls=%fused_computation.21 | custom fusion | flops 2097152 | bytes 8390660 | tf_op jit(solution)/shard_map/scatter-add | solution.py:52
  82.1 6.9 %reshape.294 = bf16[512,4096]{1,0:T(8,128)(2,1)} reshape(bf16[128,4,4096]{2,1,0:T(4,128)(2,1)} %all-gather.6.cloned.1.call-done) | data formatting | bytes 8388608
  89.0 63.4 %all-gather.4.cloned.1.call-done = bf16[4096,1024]{1,0:T(8,128)(2,1)} async-done(((bf16[32,1024]{1,0:T(8,128)(2,1)}), bf16[4096,1024]{1,0:T(8,128)(2,1)}) %all-gather.4.cloned.1.call-update) | async-done | bytes 8388624 | tf_op jit(solution)/shard_map/all_gather | solution.py:61
  152.4 18.4 %multiply_reduce_fusion = f32[1024]{0:T(1024)S(1)} fusion(bf16[1024,512]{0,1:T(8,128)(2,1)} %copy.18, bf16[512,4096]{1,0:T(8,128)(2,1)} %reshape.294, bf16[4096,1024]{1,0:T(8,128)(2,1)} %all-gather.4.cloned.1.call-done, bf16[1024,512]{1,0:T(8,128)(2,1)S(1)} %gather_fusion.1, bf16[1024,512]{1,0:T(8,128)(2,1)} %get-tuple-element.4), kind=kOutput, calls=%fused_computation.42 | convolution fusion | flops 12928416768 | bytes 15732736 | tf_op jit(solution)/shard_map/dot_general | solution.py:66
  170.8 0.7 div.84
  171.5 5.4 %all-to-all-start.1 = ((f32[128,1,8]{2,1,0:T(1,128)}), f32[128,1,8]{2,1,0:T(1,128)S(1)}, u32[]{:S(2)}, u32[]{:S(2)}) async-start(f32[128,1,8]{2,1,0:T(1,128)} %bitcast.12), calls=%async_computation.1 | async-start | bytes 131072 | tf_op jit(solution)/shard_map/all_to_all | solution.py:73
  176.9 6.0 %fusion.10 = f32[2048,512]{1,0:T(8,128)} fusion(f32[2048,512]{1,0:T(8,128)} %param.9, f32[2049,512]{1,0:T(8,128)} %scatter_custom_fusion.1, f32[2048]{0:T(1024)S(1)} %fusion.45), kind=kLoop, calls=%fused_computation.18 | loop fusion | flops 2097152 | bytes 12591104 | tf_op jit(solution)/shard_map/add | solution.py:56
  182.9 3.4 %all-to-all-done.1 = f32[128,1,8]{2,1,0:T(1,128)S(1)} async-done(((f32[128,1,8]{2,1,0:T(1,128)}), f32[128,1,8]{2,1,0:T(1,128)S(1)}, u32[]{:S(2)}, u32[]{:S(2)}) %all-to-all-start.1) | async-done | bytes 4128 | tf_op jit(solution)/shard_map/all_to_all | solution.py:73
  186.8 0.8 reduce.11
  187.7 3.4 %gather_fusion.3 = f32[512]{0:T(512)} fusion(f32[1024]{0:T(1024)S(1)} %reshape.234, s32[1024]{0:T(1024)S(1)} %pad_clamp_fusion), kind=kCustom, calls=%fused_computation.3 | custom fusion | bytes 6144 | tf_op jit(solution)/shard_map/gather | solution.py:76
  (38 shorter events, 3.7 us)
Async XLA Ops:
  7.2 57.7 %copy-start = (bf16[512,1536]{1,0:T(8,128)(2,1)S(1)}, bf16[512,1536]{1,0:T(8,128)(2,1)}, u32[]{:S(2)}) copy-start(bf16[512,1536]{1,0:T(8,128)(2,1)} %param.14) | copy-start | bytes 4718596
  7.2 9.1 %copy-start.3 = (s32[512]{0:T(512)S(1)}, s32[512]{0:T(512)}, u32[]{:S(2)}) copy-start(s32[512]{0:T(512)} %param.12) | copy-start | bytes 6148
  7.2 74.9 %all-gather.6.cloned.1.call-start = ((), (), s32[]{:S(2)}) async-start(), calls=%async_computation.3 | async-start | bytes 4227072 | tf_op jit(solution)/shard_map/all_gather | solution.py:68
  7.9 144.4 %all-gather.4.cloned.1.call-start = ((), (), s32[]{:S(2)}) async-start(), calls=%async_computation.2 | async-start | bytes 8454144 | tf_op jit(solution)/shard_map/all_gather | solution.py:61
  19.8 20.8 %all-to-all-start = ((s32[128,1,8]{2,1,0:T(1,128)}), s32[128,1,8]{2,1,0:T(1,128)S(1)}, u32[]{:S(2)}, u32[]{:S(2)}) async-start(s32[128,1,8]{2,1,0:T(1,128)} %bitcast.7), calls=%async_computation | async-start | bytes 131072 | tf_op jit(solution)/shard_map/all_to_all | solution.py:42
  64.9 1.8 copy-start.1
  64.9 2.0 %copy-start.2 = (bf16[512,1536]{1,0:T(8,128)(2,1)S(1)}, bf16[512,1536]{1,0:T(8,128)(2,1)}, u32[]{:S(2)}) copy-start(bf16[512,1536]{1,0:T(8,128)(2,1)} %param.15) | copy-start | bytes 4718596
  171.5 14.8 %all-to-all-start.1 = ((f32[128,1,8]{2,1,0:T(1,128)}), f32[128,1,8]{2,1,0:T(1,128)S(1)}, u32[]{:S(2)}, u32[]{:S(2)}) async-start(f32[128,1,8]{2,1,0:T(1,128)} %bitcast.12), calls=%async_computation.1 | async-start | bytes 131072 | tf_op jit(solution)/shard_map/all_to_all | solution.py:73
Sparse Core Ops, SparseCore 0:
  11.2 70.5 all-gather.5
  84.8 67.5 all-gather.3
where the time goes:
time: 199 us; the launch traced here: 198 us
  waiting for transfers between devices  77.5 us (39%)
  local copies, waits for them, and re-layouts  37.9 us (19%)
  other arithmetic  29.4 us (15%)
  matrix products  22 us (11%)
  starting transfers between devices  17 us (9%)
  between operations  14.3 us (7%)
    all_gather x1, waiting for transfers between devices, per_device(): lax.all_gather(tower_in, AXES, axis=0, tiled=True)  63.4 us
    dot_general x1, matrix products, per_device(): lax.dot_general(hidden, lax.all_gather(tower_out, AXES, axis=0, tiled=Tru...  18.4 us
    all_to_all x1, starting transfers between devices, per_device(): lax.all_to_all(requests, AXES, split_axis=0, concat_axis=0, tiled=True)  11.5 us
    scatter-add x1, other arithmetic, per_device(): jax.ops.segment_sum(delta, ids, num_segments=row_count + 1)[:row_count]  10.3 us
    all_to_all x1, waiting for transfers between devices, per_device(): lax.all_to_all(requests, AXES, split_axis=0, concat_axis=0, tiled=True)  9.32 us
    gather x2, local copies, waits for them, and re-layouts, per_device(): inputs = feature_table[owned_feature]  8.05 us
    gather x1, local copies, waits for them, and re-layouts, per_device(): prior = states[owned_row].astype(jnp.bfloat16)  7.46 us
    unnamed x10, local copies, waits for them, and re-layouts  7.12 us
  transfers between devices with their start and end apart: 4, of which 3 were waited for; matrix products, arithmetic and copies ran while one was open for 32% of the time, Pallas kernels for 0%

commit v1 on v0

--- a/solution.py
+++ b/solution.py
@@ -58,7 +58,9 @@
     hidden = jax.nn.gelu(
         lax.dot_general(
             joined,
-            lax.all_gather(tower_in, AXES, axis=0, tiled=True),
+            jnp.concatenate(
+                lax.all_to_all(jnp.stack([tower_in] * lax.axis_size(AXES)), AXES, 0, 0), axis=0
+            ),
             (((1,), (1,)), ((), ())),
             preferred_element_type=jnp.float32,
         )

time: 199 us -> 238 us (1.20)
  waiting for transfers between devices: 77.5 us -> 107 us
  starting transfers between devices: 17 us -> 22.7 us
  local copies, waits for them, and re-layouts: 37.9 us -> 42.2 us
    all_gather x1, waiting for transfers between devices: 0.01 us -> 94.2 us  [per_device(): lax.all_gather(tower_out, AXES, axis=0, tiled=True)]
    all_gather x1 -> x0, waiting for transfers between devices: 63.4 us -> none  [per_device(): lax.all_gather(tower_in, AXES, axis=0, tiled=True)]
    all_to_all x0 -> x1, starting transfers between devices: none -> 5.82 us  [per_device(): lax.all_to_all(jnp.stack([tower_in] * lax.axis_size(AXES)), AXES, 0, 0)]
    another operation x3 -> x4, local copies, waits for them, and re-layouts: 0.03 us -> 4.31 us  [the longest x1 4.28 us: per_device(): jnp.stack([tower_in] * lax.axis_size(AXES))]
    unnamed x10 -> x14, local copies, waits for them, and re-layouts: 7.12 us -> 7.13 us
  transfers between devices with their start and end apart: 4 -> 4, of which waited for: 3 -> 3; matrix products, arithmetic and copies ran while one was open for 32% -> 24% of each run, Pallas kernels for 0% -> 0%
where the time goes in v1:
time: 238 us; the launch traced here: 237 us
  waiting for transfers between devices  107 us (45%)
  local copies, waits for them, and re-layouts  42.2 us (18%)
  other arithmetic  29.2 us (12%)
  starting transfers between devices  22.7 us (10%)
  matrix products  21.8 us (9%)
  between operations  14.3 us (6%)
    all_gather x1, waiting for transfers between devices, per_device(): lax.all_gather(tower_out, AXES, axis=0, tiled=True)  94.2 us
    dot_general x1, matrix products, per_device(): lax.dot_general(hidden, lax.all_gather(tower_out, AXES, axis=0, tiled=Tru...  18.2 us
    all_to_all x1, starting transfers between devices, per_device(): lax.all_to_all(requests, AXES, split_axis=0, concat_axis=0, tiled=True)  11.5 us
    scatter-add x1, other arithmetic, per_device(): jax.ops.segment_sum(delta, ids, num_segments=row_count + 1)[:row_count]  10.2 us
    all_to_all x1, waiting for transfers between devices, per_device(): lax.all_to_all(requests, AXES, split_axis=0, concat_axis=0, tiled=True)  8.59 us
    gather x2, local copies, waits for them, and re-layouts, per_device(): inputs = feature_table[owned_feature]  8.05 us
    gather x1, local copies, waits for them, and re-layouts, per_device(): prior = states[owned_row].astype(jnp.bfloat16)  7.46 us
    unnamed x14, local copies, waits for them, and re-layouts  7.13 us
  transfers between devices with their start and end apart: 4, of which 3 were waited for; matrix products, arithmetic and copies ran while one was open for 24% of the time, Pallas kernels for 0%

profile of v1, /device:TPU:1, one launch (start us, length us, event | category | flops | bytes accessed | tf_op | source)
XLA Modules:
  0.0 237.0 jit_solution(8702147537769729699)
XLA Ops:
  7.2 0.8 compare_select_fusion.8
  8.0 6.5 %gather_fusion = s32[512]{0:T(512)S(1)} fusion(s32[262144]{0:T(1024)} %param.10, s32[1024]{0:T(1024)S(1)} %pad_clamp_fusion.1), kind=kCustom, calls=%fused_computation | custom fusion | bytes 6144 | tf_op jit(solution)/shard_map/gather | solution.py:34
  15.3 2.4 %scatter_custom_fusion = s32[1024]{0:T(1024)S(1)} fusion(s32[512]{0:T(512)S(1)} %bitcast.52, s32[512]{0:T(512)S(1)} %get-tuple-element.10, s32[]{:T(128)} %constant.20.clone.1), kind=kCustom, calls=%fused_computation.94 | custom fusion | bytes 4100 | tf_op jit(solution)/shard_map/scatter | solution.py:41
  18.4 11.5 %all-to-all-start = ((s32[128,1,8]{2,1,0:T(1,128)}), s32[128,1,8]{2,1,0:T(1,128)S(1)}, u32[]{:S(2)}, u32[]{:S(2)}) async-start(s32[128,1,8]{2,1,0:T(1,128)} %bitcast.7), calls=%async_computation | async-start | bytes 131072 | tf_op jit(solution)/shard_map/all_to_all | solution.py:42
  30.7 8.6 %all-to-all-done = s32[128,1,8]{2,1,0:T(1,128)S(1)} async-done(((s32[128,1,8]{2,1,0:T(1,128)}), s32[128,1,8]{2,1,0:T(1,128)S(1)}, u32[]{:S(2)}, u32[]{:S(2)}) %all-to-all-start) | async-done | bytes 4128 | tf_op jit(solution)/shard_map/all_to_all | solution.py:42
  39.3 4.3 %stack.2 = bf16[128,32,1024]{2,1,0:T(8,128)(2,1)} broadcast(bf16[32,1024]{1,0:T(8,128)(2,1)S(1)} %copy-done.4), dimensions={1,2} | broadcast | bytes 8454144 | tf_op jit(solution)/shard_map/stack | solution.py:62
  43.5 5.8 %all-to-all-start.1 = ((bf16[128,32,1024]{2,1,0:T(8,128)(2,1)}), bf16[128,32,1024]{2,1,0:T(8,128)(2,1)}, u32[]{:S(2)}, u32[]{:S(2)}) async-start(bf16[128,32,1024]{2,1,0:T(8,128)(2,1)} %stack.2), calls=%async_computation.1 | async-start | bytes 16777216 | tf_op jit(solution)/shard_map/all_to_all | solution.py:62
  49.9 1.0 fusion.44
  51.0 6.7 %gather_fusion.1 = bf16[1024,512]{1,0:T(8,128)(2,1)S(1)} fusion(bf16[4096,512]{1,0:T(8,128)(2,1)} %param.13, s32[1024]{0:T(1024)S(1)} %broadcast_clamp_fusion.1), kind=kCustom, calls=%fused_computation.1 | custom fusion | bytes 2101248 | tf_op jit(solution)/shard_map/gather | solution.py:48
  57.8 1.3 copy.18
  59.2 7.5 %gather_fusion.2 = f32[1024,512]{1,0:T(8,128)} fusion(f32[2048,512]{1,0:T(8,128)} %param.9, s32[1024]{0:T(1024)S(1)} %broadcast_clamp_fusion), kind=kCustom, calls=%fused_computation.2 | custom fusion | bytes 4198400 | tf_op jit(solution)/shard_map/gather | solution.py:47
  66.7 6.9 %scatter_custom_fusion.2 = s32[2049]{0:T(1024)S(1)} fusion(s32[1024]{0:T(1024)S(1)} %bitcast.54, s32[1024]{0:T(1024)S(1)} %reshape.294, s32[]{:T(128)} %constant.21.clone.1), kind=kCustom, calls=%fused_computation.66 | custom fusion | flops 1024 | bytes 8200 | tf_op jit(solution)/shard_map/scatter-add | solution.py:53
  73.7 1.8 fusion.66
  75.7 1.8 fusion.61
  77.5 2.9 %fusion.64 = (bf16[1024,512]{1,0:T(8,128)(2,1)S(1)}, f32[1024,512]{1,0:T(8,128)}) fusion(f32[1024,512]{1,0:T(8,128)S(1)} %copy-done.2, f32[1024,1536]{1,0:T(8,128)S(1)} %fusion.61, f32[1024,1536]{1,0:T(8,128)S(1)} %fusion.66), kind=kLoop, calls=%fused_computation.106 | loop fusion | flops 8912896 | bytes 17825792 | tf_op jit(solution)/shard_map/convert_element_type | solution.py:57
  80.3 10.2 %scatter_custom_fusion.1 = f32[2049,512]{1,0:T(8,128)} fusion(s32[1024]{0:T(1024)S(1)} %bitcast.55, f32[]{:T(128)} %constant.19.clone.1, f32[1024,512]{1,0:T(8,128)} %get-tuple-element.5, f32[1024,512]{1,0:T(8,128)} %gather_fusion.2), kind=kCustom, calls=%fused_computation.21 | custom fusion | flops 2097152 | bytes 8390660 | tf_op jit(solution)/shard_map/scatter-add | solution.py:52
  90.5 94.2 %all-gather.3.cloned.1.call-done = bf16[128,4,4096]{2,1,0:T(4,128)(2,1)} async-done(((bf16[1,4,4096]{2,1,0:T(4,128)(2,1)}), bf16[128,4,4096]{2,1,0:T(4,128)(2,1)}) %all-gather.3.cloned.1.call-update) | async-done | bytes 4194320 | tf_op jit(solution)/shard_map/all_gather | solution.py:70
  184.7 6.9 %reshape.300 = bf16[512,4096]{1,0:T(8,128)(2,1)} reshape(bf16[128,4,4096]{2,1,0:T(4,128)(2,1)} %all-gather.3.cloned.1.call-done) | data formatting | bytes 8388608
  191.6 18.2 %multiply_reduce_fusion = f32[1024]{0:T(1024)S(1)} fusion(bf16[1024,512]{0,1:T(8,128)(2,1)} %copy.18, bf16[512,4096]{1,0:T(8,128)(2,1)} %reshape.300, bf16[4096,1024]{1,0:T(8,128)(2,1)} %bitcast.11, bf16[1024,512]{1,0:T(8,128)(2,1)S(1)} %gather_fusion.1, bf16[1024,512]{1,0:T(8,128)(2,1)S(1)} %get-tuple-element.4), kind=kOutput, calls=%fused_computation.42 | convolution fusion | flops 12928416768 | bytes 15732736 | tf_op jit(solution)/shard_map/dot_general | solution.py:68
  210.5 5.3 %all-to-all-start.2 = ((f32[128,1,8]{2,1,0:T(1,128)}), f32[128,1,8]{2,1,0:T(1,128)S(1)}, u32[]{:S(2)}, u32[]{:S(2)}) async-start(f32[128,1,8]{2,1,0:T(1,128)} %bitcast.13), calls=%async_computation.2 | async-start | bytes 131072 | tf_op jit(solution)/shard_map/all_to_all | solution.py:75
  215.9 6.1 %fusion.10 = f32[2048,512]{1,0:T(8,128)} fusion(f32[2048,512]{1,0:T(8,128)} %param.9, f32[2049,512]{1,0:T(8,128)} %scatter_custom_fusion.1, f32[2048]{0:T(1024)S(1)} %fusion.45), kind=kLoop, calls=%fused_computation.18 | loop fusion | flops 2097152 | bytes 12591104 | tf_op jit(solution)/shard_map/add | solution.py:56
  222.0 3.3 %all-to-all-done.2 = f32[128,1,8]{2,1,0:T(1,128)S(1)} async-done(((f32[128,1,8]{2,1,0:T(1,128)}), f32[128,1,8]{2,1,0:T(1,128)S(1)}, u32[]{:S(2)}, u32[]{:S(2)}) %all-to-all-start.2) | async-done | bytes 4128 | tf_op jit(solution)/shard_map/all_to_all | solution.py:75
  225.8 0.8 reduce.11
  226.7 3.4 %gather_fusion.3 = f32[512]{0:T(512)} fusion(f32[1024]{0:T(1024)S(1)} %reshape.240, s32[1024]{0:T(1024)S(1)} %pad_clamp_fusion), kind=kCustom, calls=%fused_computation.3 | custom fusion | bytes 6144 | tf_op jit(solution)/shard_map/gather | solution.py:78
  (42 shorter events, 4.5 us)
Async XLA Ops:
  7.2 66.5 %copy-start = (bf16[512,1536]{1,0:T(8,128)(2,1)S(1)}, bf16[512,1536]{1,0:T(8,128)(2,1)}, u32[]{:S(2)}) copy-start(bf16[512,1536]{1,0:T(8,128)(2,1)} %param.14) | copy-start | bytes 4718596
  7.2 7.8 %copy-start.5 = (s32[512]{0:T(512)S(1)}, s32[512]{0:T(512)}, u32[]{:S(2)}) copy-start(s32[512]{0:T(512)} %param.12) | copy-start | bytes 6148
  7.2 32.1 %copy-start.4 = (bf16[32,1024]{1,0:T(8,128)(2,1)S(1)}, bf16[32,1024]{1,0:T(8,128)(2,1)}, u32[]{:S(2)}) copy-start(bf16[32,1024]{1,0:T(8,128)(2,1)} %param.16) | copy-start | bytes 196612
  18.4 20.8 %all-to-all-start = ((s32[128,1,8]{2,1,0:T(1,128)}), s32[128,1,8]{2,1,0:T(1,128)S(1)}, u32[]{:S(2)}, u32[]{:S(2)}) async-start(s32[128,1,8]{2,1,0:T(1,128)} %bitcast.7), calls=%async_computation | async-start | bytes 131072 | tf_op jit(solution)/shard_map/all_to_all | solution.py:42
  29.9 154.8 %all-gather.3.cloned.1.call-start = ((), (), s32[]{:S(2)}) async-start(), calls=%async_computation.3 | async-start | bytes 4227072 | tf_op jit(solution)/shard_map/all_gather | solution.py:70
  43.5 148.1 %all-to-all-start.1 = ((bf16[128,32,1024]{2,1,0:T(8,128)(2,1)}), bf16[128,32,1024]{2,1,0:T(8,128)(2,1)}, u32[]{:S(2)}, u32[]{:S(2)}) async-start(bf16[128,32,1024]{2,1,0:T(8,128)(2,1)} %stack.2), calls=%async_computation.1 | async-start | bytes 16777216 | tf_op jit(solution)/shard_map/all_to_all | solution.py:62
  73.6 1.8 copy-start.2
  73.7 2.0 copy-start.3
  210.5 14.7 %all-to-all-start.2 = ((f32[128,1,8]{2,1,0:T(1,128)}), f32[128,1,8]{2,1,0:T(1,128)S(1)}, u32[]{:S(2)}, u32[]{:S(2)}) async-start(f32[128,1,8]{2,1,0:T(1,128)} %bitcast.13), calls=%async_computation.2 | async-start | bytes 131072 | tf_op jit(solution)/shard_map/all_to_all | solution.py:75
  215.9 14.2 %copy-start.1 = (bf16[512,1536]{1,0:T(8,128)(2,1)S(1)}, bf16[512,1536]{1,0:T(8,128)(2,1)}, u32[]{:S(2)}) copy-start(bf16[512,1536]{1,0:T(8,128)(2,1)} %param.14) | copy-start | bytes 4718596
Sparse Core Ops, SparseCore 0:
  33.9 150.7 all-gather.2
